TPU v7x, 32 devices: a whole 2x2x4 slice. The times are simulated.
32 devices in a mesh: rep: 4 (over x, core), ep: 4 (over z), grp: 2 (over y).
Axes of the slice: x: 2, y: 2, z: 4, core: 2. Of those that a mesh axis runs over, the one named last changes fastest.
Arguments:
- tokens: bfloat16 [4096, 2048], P(('rep', 'ep', 'grp')), may hold values from -6 to 6
- grad_out: bfloat16 [4096, 2048], P(('rep', 'ep', 'grp')), may hold values from -6 to 6
- expert_ids: int32 [4096, 2], P(('rep', 'ep', 'grp')), may hold values from 0 to 7, as said below
- combine: bfloat16 [4096, 2], P(('rep', 'ep', 'grp')), may hold values from 0.099609375 to 1
- weights: bfloat16 [2048, 3, 7168], P('grp', None, 'ep'), may hold values from -0.125 to 0.125
Outputs:
- grad_tokens: bfloat16 [4096, 2048], P(('rep', 'ep', 'grp'))
- grad_combine: float32 [4096, 2], P(('rep', 'ep', 'grp'))
- grad_weights: float32 [2048, 3, 7168], P(('rep', 'grp'), None, 'ep')
Inputs may be any that keep to these rules, and one draw needn't show every extreme that they name: `expert_ids`: each token names 2 different experts, at most one of them below 1. No expert below 1 is named by more than 4 tokens of one device, and each of them is named by exactly 4 tokens of some device.
All inputs are finite; a program needn't handle non-finite values.
Results may differ from a plain program's by a relative error of at most 0.0085.
Values may be sent and summed in bfloat16 or wider, within the bound.
A program may use at most 128 MiB of HBM per device.

v0:
```python
import jax
import jax.numpy as jnp
from jax import lax
from jax.sharding import PartitionSpec as P

FLIGHT = 1
CAP = 4


def route_slots(routing, gate_vals, in_flight, capacity):
    experts = jnp.arange(in_flight, dtype=jnp.int32)
    matches = (routing[None, :, :] == experts[:, None, None]).astype(jnp.float32)
    assigned = jnp.sum(matches, axis=2)
    combined = jnp.sum(matches * gate_vals.astype(jnp.float32)[None, :, :], axis=2)
    before = jnp.cumsum(assigned, axis=1) - assigned
    slot_index = jnp.arange(capacity, dtype=jnp.float32)
    slot_map = (before[:, None, :] == slot_index[None, :, None]).astype(jnp.float32) * assigned[
        :, None, :
    ]
    return (matches, combined, slot_map)


def local(tokens, grad_out, expert_ids, combine, weights):
    ep_size = lax.axis_size("ep")
    rep_size = lax.axis_size("rep")
    grp_size = lax.axis_size("grp")
    quarter = ep_size // FLIGHT
    model_width = tokens.shape[1]
    slot_total = ep_size * CAP
    owner_rows = model_width // (rep_size * grp_size)
    highest = lax.Precision.HIGHEST
    matches, combined, slot_map = route_slots(expert_ids, combine, FLIGHT, CAP)
    slot_bf = slot_map.astype(jnp.bfloat16)
    sent_rows = jnp.einsum(
        "fct,td->fcd", slot_bf, tokens, preferred_element_type=jnp.float32
    ).astype(jnp.bfloat16)
    sent_grads = jnp.einsum(
        "fct,td->fcd", slot_bf, grad_out, preferred_element_type=jnp.float32
    ).astype(jnp.bfloat16)
    sent_scale = jnp.einsum("fct,ft->fc", slot_map, combined, precision=highest).astype(
        jnp.bfloat16
    )

    def spread(buffer):
        trailing = buffer.shape[1:]
        widened = jnp.broadcast_to(buffer[:, None], (FLIGHT, quarter) + trailing)
        return widened.reshape((ep_size,) + trailing)

    recv_rows, recv_grads, recv_scale = (
        lax.all_to_all(spread(sent_rows), "ep", split_axis=0, concat_axis=0, tiled=True),
        lax.all_to_all(spread(sent_grads), "ep", split_axis=0, concat_axis=0, tiled=True),
        lax.all_to_all(spread(sent_scale), "ep", split_axis=0, concat_axis=0, tiled=True),
    )
    token_rows = recv_rows.reshape(slot_total, model_width)
    grad_rows = recv_grads.reshape(slot_total, model_width)
    row_scale = recv_scale.reshape(slot_total, 1).astype(jnp.float32)

    def owner_layout(rows_now):
        shaped = rows_now.reshape(slot_total, rep_size, grp_size, owner_rows)
        return jnp.transpose(shaped, (2, 0, 1, 3))

    col_tokens, col_grads = (
        lax.all_to_all(owner_layout(token_rows), "grp", split_axis=0, concat_axis=0, tiled=True),
        lax.all_to_all(owner_layout(grad_rows), "grp", split_axis=0, concat_axis=0, tiled=True),
    )
    col_tokens = col_tokens.reshape(grp_size * slot_total, rep_size * owner_rows)
    col_grads = col_grads.reshape(grp_size * slot_total, rep_size * owner_rows)
    gathered = lax.all_gather(weights, "grp", axis=0, tiled=True)
    gate_up_pre = jnp.einsum(
        "rd,dkh->rkh", token_rows, gathered[:, :2], preferred_element_type=jnp.float32
    )
    down_back = jnp.dot(grad_rows, gathered[:, 2], preferred_element_type=jnp.float32)
    gate_pre = gate_up_pre[:, 0]
    up_pre = gate_up_pre[:, 1]
    sigmoid_gate = jax.nn.sigmoid(gate_pre)
    activated = gate_pre * sigmoid_gate
    hid_value = activated * up_pre
    hid_grad = row_scale * down_back
    grad_gate = (hid_grad * up_pre * sigmoid_gate * (1.0 + gate_pre * (1.0 - sigmoid_gate))).astype(
        jnp.bfloat16
    )
    grad_up = (hid_grad * activated).astype(jnp.bfloat16)
    scaled_hid = (row_scale * hid_value).astype(jnp.bfloat16)
    gate_up_grad = jnp.stack([grad_gate, grad_up], axis=1)
    hidden_all = jnp.stack([grad_gate, grad_up, scaled_hid], axis=1)
    partial_c = jnp.sum(hid_value * down_back, axis=1).astype(jnp.bfloat16)
    partial_x = jnp.einsum(
        "rkh,dkh->rd", gate_up_grad, gathered[:, :2], preferred_element_type=jnp.float32
    )
    back_x, back_c = (
        lax.all_to_all(
            partial_x.astype(jnp.bfloat16).reshape(ep_size, CAP, model_width),
            "ep",
            split_axis=0,
            concat_axis=0,
            tiled=True,
        ),
        lax.all_to_all(
            partial_c.reshape(ep_size, CAP), "ep", split_axis=0, concat_axis=0, tiled=True
        ),
    )
    summed_x = jnp.sum(
        back_x.astype(jnp.float32).reshape(FLIGHT, quarter, CAP, model_width), axis=1
    )
    summed_c = jnp.sum(back_c.astype(jnp.float32).reshape(FLIGHT, quarter, CAP), axis=1)
    grad_tokens = jnp.einsum("fct,fcd->td", slot_map, summed_x, precision=highest).astype(
        jnp.bfloat16
    )
    per_token = jnp.einsum("fct,fc->ft", slot_map, summed_c, precision=highest)
    grad_combine = jnp.sum(matches * per_token[:, :, None], axis=0)
    hidden_grads = lax.all_gather(hidden_all, "grp", axis=0, tiled=True)
    gate_up_term = jnp.einsum(
        "rc,rkh->ckh", col_tokens, hidden_grads[:, :2], preferred_element_type=jnp.float32
    )
    down_term = jnp.einsum(
        "rc,rh->ch", col_grads, hidden_grads[:, 2], preferred_element_type=jnp.float32
    )
    grad_weights = lax.psum_scatter(
        jnp.concatenate([gate_up_term, down_term[:, None, :]], axis=1).astype(jnp.bfloat16),
        "rep",
        scatter_dimension=0,
        tiled=True,
    ).astype(jnp.float32)
    return (grad_tokens, grad_combine, grad_weights)


def solution(mesh):
    in_specs = (
        P(("rep", "ep", "grp"), None),
        P(("rep", "ep", "grp"), None),
        P(("rep", "ep", "grp"), None),
        P(("rep", "ep", "grp"), None),
        P("grp", None, "ep"),
    )
    out_specs = (
        P(("rep", "ep", "grp"), None),
        P(("rep", "ep", "grp"), None),
        P(("rep", "grp"), None, "ep"),
    )
    return jax.shard_map(local, mesh=mesh, in_specs=in_specs, out_specs=out_specs, check_vma=False)
```

profile of v0, /device:TPU:0, one launch (start us, length us, event | category | flops | bytes accessed | tf_op | source)
XLA Modules:
  0.0 396.5 jit_solution(2041849928835757291)
XLA Ops:
  7.3 0.7 all-gather.2.cloned.1.call-update
  8.5 0.6 reshape.246
  9.1 6.3 %all-to-all-start = ((bf16[4,1,4]{2,1,0:T(2,128)(2,1)}), bf16[4,1,4]{2,1,0:T(2,128)(2,1)S(1)}, u32[]{:S(2)}, u32[]{:S(2)}) async-start(bf16[4,1,4]{2,1,0:T(2,128)(2,1)} %reshape.246), calls=%async_computation | async-start | bytes 4096 | tf_op jit(solution)/shard_map/all_to_all | solution.py:52
  15.7 5.3 %all-to-all-done = bf16[4,1,4]{2,1,0:T(2,128)(2,1)S(1)} async-done(((bf16[4,1,4]{2,1,0:T(2,128)(2,1)}), bf16[4,1,4]{2,1,0:T(2,128)(2,1)S(1)}, u32[]{:S(2)}, u32[]{:S(2)}) %all-to-all-start) | async-done | bytes 64 | tf_op jit(solution)/shard_map/all_to_all | solution.py:52
  21.0 0.6 reshape.247
  21.6 3.3 all-to-all-start.1
  25.1 5.5 %all-to-all-done.1 = bf16[4,4,2048]{2,1,0:T(4,128)(2,1)S(1)} async-done(((bf16[4,4,2048]{2,1,0:T(4,128)(2,1)}), bf16[4,4,2048]{2,1,0:T(4,128)(2,1)S(1)}, u32[]{:S(2)}, u32[]{:S(2)}) %all-to-all-start.1) | async-done | bytes 65568 | tf_op jit(solution)/shard_map/all_to_all | solution.py:51
  30.6 0.6 reshape.249
  31.3 3.3 all-to-all-start.2
  34.6 0.7 copy.18
  35.3 5.0 %all-to-all-done.2 = bf16[4,4,2048]{2,1,0:T(4,128)(2,1)S(1)} async-done(((bf16[4,4,2048]{2,1,0:T(4,128)(2,1)}), bf16[4,4,2048]{2,1,0:T(4,128)(2,1)S(1)}, u32[]{:S(2)}, u32[]{:S(2)}) %all-to-all-start.2) | async-done | bytes 65568 | tf_op jit(solution)/shard_map/all_to_all | solution.py:50
  40.3 3.3 all-to-all-start.6
  43.7 0.7 copy.21
  44.3 4.2 %all-to-all-done.6 = bf16[2,16,4,256]{3,2,1,0:T(4,128)(2,1)S(1)} async-done(((bf16[2,16,4,256]{3,2,1,0:T(4,128)(2,1)}), bf16[2,16,4,256]{3,2,1,0:T(4,128)(2,1)S(1)}, u32[]{:S(2)}, u32[]{:S(2)}) %all-to-all-start.6) | async-done | bytes 65568 | tf_op jit(solution)/shard_map/all_to_all | solution.py:64
  48.5 3.3 all-to-all-start.5
  52.1 4.7 %all-to-all-done.5 = bf16[2,16,4,256]{3,2,1,0:T(4,128)(2,1)S(1)} async-done(((bf16[2,16,4,256]{3,2,1,0:T(4,128)(2,1)}), bf16[2,16,4,256]{3,2,1,0:T(4,128)(2,1)S(1)}, u32[]{:S(2)}, u32[]{:S(2)}) %all-to-all-start.5) | async-done | bytes 65568 | tf_op jit(solution)/shard_map/all_to_all | solution.py:63
  56.8 215.1 %all-gather.2.cloned.1.call-done = bf16[2048,3,1792]{2,0,1:T(8,128)(2,1)} async-done(((bf16[1024,3,1792]{2,0,1:T(8,128)(2,1)}), bf16[2048,3,1792]{2,0,1:T(8,128)(2,1)}) %all-gather.2.cloned.1.call-update) | async-done | bytes 22020112 | tf_op jit(solution)/shard_map/all_gather | solution.py:68
  271.9 6.2 %fusion.2 = f32[16,2,1792]{2,0,1:T(8,128)S(1)} fusion(bf16[16,2048,1]{1,0,2:T(8,128)(2,1)S(1)} %reshape.257, bf16[2048,3,1792]{2,0,1:T(8,128)(2,1)} %all-gather.2.cloned.1.call-done), kind=kOutput, calls=%fused_computation.2 | convolution fusion | flops 234881024 | bytes 14974976 | tf_op jit(solution)/shard_map/rd,dkh->rkh/dot_general | solution.py:69
  278.2 4.3 %fusion.27 = (bf16[16,1,1792]{2,0,1:T(8,128)(2,1)S(1)}, bf16[16,1,1792]{2,0,1:T(8,128)(2,1)S(1)}, bf16[16]{0:T(256)(128)(2,1)S(1)}) fusion(f32[16,2,1792]{2,0,1:T(8,128)S(1)} %fusion.2, f32[16]{0:T(128)S(1)} %reshape.254, bf16[16,2048]{1,0:T(8,128)(2,1)S(1)} %reshape.248, bf16[2048,3,1792]{2,0,1:T(8,128)(2,1)} %all-gather.2.cloned.1.call-done), kind=kOutput, calls=%fused_computation.43 | convolution fusion | flops 117927920 | bytes 7749728 | tf_op jit(solution)/shard_map/dot_general | solution.py:72
  282.5 6.6 %all_gather.7 = bf16[32,3,1792]{2,0,1:T(8,128)(2,1)S(1)} all-gather(bf16[16,3,1792]{2,0,1:T(8,128)(2,1)S(1)} %pad_maximum_fusion.1), channel_id=1, replica_groups=mesh['rep'=4,'ep'=4,'grp'=2] {'grp'}, dimensions={0}, use_global_device_ids=true | all-gather | bytes 516096 | tf_op jit(solution)/shard_map/all_gather | solution.py:111
  289.1 1.1 fusion.5
  290.3 2.1 convolution_convert_fusion
  292.4 4.9 %pad_maximum_fusion = bf16[1024,3,1792]{2,0,1:T(8,128)(2,1)} fusion(bf16[1024,1,1792]{2,0,1:T(8,128)(2,1)S(1)} %fusion.5, bf16[1024,2,1792]{2,0,1:T(8,128)(2,1)S(1)} %convolution_convert_fusion), kind=kLoop, calls=%fused_computation.4 | loop fusion | flops 5505024 | bytes 22020096 | tf_op jit(solution)/shard_map/concatenate | solution.py:119
  297.3 7.2 %fusion.9 = bf16[16,2048]{1,0:T(8,128)(2,1)S(1)} fusion(bf16[2048,3,1792]{2,0,1:T(8,128)(2,1)} %all-gather.2.cloned.1.call-done, bf16[16,1,1792]{2,0,1:T(8,128)(2,1)S(1)} %get-tuple-element.6, bf16[16,1,1792]{2,0,1:T(8,128)(2,1)S(1)} %get-tuple-element.5), kind=kOutput, calls=%fused_computation.12 | convolution fusion | flops 234971136 | bytes 14860288 | tf_op jit(solution)/shard_map/rkh,dkh->rd/dot_general | solution.py:87
  304.6 0.7 reshape.251
  305.3 10.0 %all_to_all.37 = bf16[4,1,4]{2,1,0:T(2,128)(2,1)S(1)} all-to-all(bf16[4,1,4]{2,1,0:T(2,128)(2,1)S(1)} %convert_element_type.105), channel_id=1, replica_groups=mesh['rep'=4,'ep'=4,'grp'=2] {'ep'}, dimensions={0} | all-to-all | bytes 64 | tf_op jit(solution)/shard_map/all_to_all | solution.py:98
  315.3 3.3 all-to-all-start.3
  318.7 0.6 broadcast_select_fusion
  319.3 5.0 %all-to-all-done.3 = bf16[4,4,2048]{2,1,0:T(4,128)(2,1)S(1)} async-done(((bf16[4,4,2048]{2,1,0:T(4,128)(2,1)}), bf16[4,4,2048]{2,1,0:T(4,128)(2,1)S(1)}, u32[]{:S(2)}, u32[]{:S(2)}) %all-to-all-start.3) | async-done | bytes 65568 | tf_op jit(solution)/shard_map/all_to_all | solution.py:91
  324.3 1.8 convolution_convert_fusion.2
  326.2 58.8 %reduce-scatter.2.cloned.1.call-done = bf16[256,3,1792]{2,0,1:T(8,128)(2,1)} async-done(((bf16[1024,3,1792]{2,0,1:T(8,128)(2,1)}), bf16[256,3,1792]{2,0,1:T(8,128)(2,1)}) %reduce-scatter.2.cloned.1.call-update) | async-done | bytes 2752528 | tf_op jit(solution)/shard_map/reduce_scatter | solution.py:118
  385.0 4.7 %convert_element_type.103 = f32[256,3,1792]{2,0,1:T(8,128)} convert(bf16[256,3,1792]{2,0,1:T(8,128)(2,1)} %reduce-scatter.2.cloned.1.call-done) | non-fusion elementwise | flops 1376256 | bytes 8257536 | tf_op jit(solution)/shard_map/convert_element_type | solution.py:123
  (35 shorter events, 1.7 us)
Async XLA Ops:
  7.2 8.3 %copy-start = (bf16[128,2048]{1,0:T(8,128)(2,1)S(1)}, bf16[128,2048]{1,0:T(8,128)(2,1)}, u32[]{:S(2)}) copy-start(bf16[128,2048]{1,0:T(8,128)(2,1)} %param.6) | copy-start | bytes 1572868
  7.2 0.8 copy-start.3
  7.2 0.8 copy-start.4
  7.2 17.7 %copy-start.2 = (bf16[128,2048]{1,0:T(8,128)(2,1)S(1)}, bf16[128,2048]{1,0:T(8,128)(2,1)}, u32[]{:S(2)}) copy-start(bf16[128,2048]{1,0:T(8,128)(2,1)} %param.5) | copy-start | bytes 1572868
  7.2 264.7 %all-gather.2.cloned.1.call-start = ((), (), s32[]{:S(2)}) async-start(), calls=%async_computation.8 | async-start | bytes 33030144 | tf_op jit(solution)/shard_map/all_gather | solution.py:68
  9.1 11.8 %all-to-all-start = ((bf16[4,1,4]{2,1,0:T(2,128)(2,1)}), bf16[4,1,4]{2,1,0:T(2,128)(2,1)S(1)}, u32[]{:S(2)}, u32[]{:S(2)}) async-start(bf16[4,1,4]{2,1,0:T(2,128)(2,1)} %reshape.246), calls=%async_computation | async-start | bytes 4096 | tf_op jit(solution)/shard_map/all_to_all | solution.py:52
  21.6 9.0 %all-to-all-start.1 = ((bf16[4,4,2048]{2,1,0:T(4,128)(2,1)}), bf16[4,4,2048]{2,1,0:T(4,128)(2,1)S(1)}, u32[]{:S(2)}, u32[]{:S(2)}) async-start(bf16[4,4,2048]{2,1,0:T(4,128)(2,1)} %reshape.247), calls=%async_computation.1 | async-start | bytes 131072 | tf_op jit(solution)/shard_map/all_to_all | solution.py:51
  31.3 9.0 %all-to-all-start.2 = ((bf16[4,4,2048]{2,1,0:T(4,128)(2,1)}), bf16[4,4,2048]{2,1,0:T(4,128)(2,1)S(1)}, u32[]{:S(2)}, u32[]{:S(2)}) async-start(bf16[4,4,2048]{2,1,0:T(4,128)(2,1)} %reshape.249), calls=%async_computation.2 | async-start | bytes 131072 | tf_op jit(solution)/shard_map/all_to_all | solution.py:50
  40.3 8.2 %all-to-all-start.6 = ((bf16[2,16,4,256]{3,2,1,0:T(4,128)(2,1)}), bf16[2,16,4,256]{3,2,1,0:T(4,128)(2,1)S(1)}, u32[]{:S(2)}, u32[]{:S(2)}) async-start(bf16[2,16,4,256]{3,2,1,0:T(4,128)(2,1)} %copy.18), calls=%async_computation.6 | async-start | bytes 131072 | tf_op jit(solution)/shard_map/all_to_all | solution.py:64
  48.5 8.2 %all-to-all-start.5 = ((bf16[2,16,4,256]{3,2,1,0:T(4,128)(2,1)}), bf16[2,16,4,256]{3,2,1,0:T(4,128)(2,1)S(1)}, u32[]{:S(2)}, u32[]{:S(2)}) async-start(bf16[2,16,4,256]{3,2,1,0:T(4,128)(2,1)} %bitcast.83), calls=%async_computation.5 | async-start | bytes 131072 | tf_op jit(solution)/shard_map/all_to_all | solution.py:63
  51.8 333.1 %reduce-scatter.2.cloned.1.call-start = ((), (), s32[]{:S(2)}) async-start(), calls=%async_computation.9 | async-start | bytes 13762560 | tf_op jit(solution)/shard_map/reduce_scatter | solution.py:118
  297.3 92.4 %copy-start.1 = (bf16[128,2048]{1,0:T(8,128)(2,1)S(1)}, bf16[128,2048]{1,0:T(8,128)(2,1)}, u32[]{:S(2)}) copy-start(bf16[128,2048]{1,0:T(8,128)(2,1)} %param.6) | copy-start | bytes 1572868
  315.3 9.0 %all-to-all-start.3 = ((bf16[4,4,2048]{2,1,0:T(4,128)(2,1)}), bf16[4,4,2048]{2,1,0:T(4,128)(2,1)S(1)}, u32[]{:S(2)}, u32[]{:S(2)}) async-start(bf16[4,4,2048]{2,1,0:T(4,128)(2,1)} %reshape.251), calls=%async_computation.3 | async-start | bytes 131072 | tf_op jit(solution)/shard_map/all_to_all | solution.py:91
Sparse Core Ops, SparseCore 0:
  9.6 262.2 all-gather.1
  297.4 87.5 reduce-scatter.1
where the time goes:
time: 397 us
  waiting for transfers between devices  304 us (77%)
  matrix products  23.4 us (6%)
  starting transfers between devices  22.9 us (6%)
  blocking collectives  16.6 us (4%)
  between operations  14.2 us (4%)
  other arithmetic  10.7 us (3%)
  local copies, waits for them, and re-layouts  4.37 us (1%)
    all_gather x1, waiting for transfers between devices, local(): gathered = lax.all_gather(weights, 'grp', axis=0, tiled=True)  215 us
    reduce_scatter x1, waiting for transfers between devices, local(): lax.psum_scatter(jnp.concatenate([gate_up_term, down_term[:, None, :]], a...  58.8 us
    all_to_all x1, blocking collectives, local(): lax.all_to_all(partial_c.reshape(ep_size, CAP), 'ep', split_axis=0, conca...  9.96 us
  transfers between devices with their start and end apart: 8, of which 8 were waited for; matrix products, arithmetic and copies ran while one was open for 4% of the time, Pallas kernels for 0%

commit v1 on v0

v1 whole, which is shorter than its diff:
```python
import jax
import jax.numpy as jnp
from jax import lax
from jax.sharding import PartitionSpec as P

FLIGHT = 1
CAP = 4


def route_slots(routing, gate_vals):
    match = (routing == 0).astype(jnp.float32)
    assigned = jnp.sum(match, axis=1)
    combined = jnp.sum(match * gate_vals.astype(jnp.float32), axis=1)
    before = jnp.cumsum(assigned) - assigned
    slot_index = jnp.arange(CAP, dtype=jnp.float32)
    slot_map = (before[None, :] == slot_index[:, None]).astype(jnp.float32) * assigned[None, :]
    return match, combined, slot_map


def local(tokens, grad_out, expert_ids, combine, weights):
    ep, rep, grp = lax.axis_size("ep"), lax.axis_size("rep"), lax.axis_size("grp")
    me_g = lax.axis_index("grp")
    width = tokens.shape[1]
    half = width // grp
    owner = width // (rep * grp)
    hid = weights.shape[2]
    peers = ep * grp
    rows = peers * CAP
    pad = 128
    f32, bf16 = jnp.float32, jnp.bfloat16
    match, combined, slot_map = route_slots(expert_ids, combine)
    slot_bf = slot_map.astype(bf16)
    xs = jnp.dot(slot_bf, tokens, preferred_element_type=f32).astype(bf16)
    ys = jnp.dot(slot_bf, grad_out, preferred_element_type=f32).astype(bf16)
    cs = jnp.sum(slot_map * combined[None, :], axis=1).astype(bf16)
    sent = jnp.concatenate([xs, ys, jnp.broadcast_to(cs[:, None], (CAP, pad))], axis=1)
    got = lax.all_gather(sent, ("grp", "ep"), axis=0, tiled=True)
    pair = got[:, : 2 * width].reshape(rows, 2, width)
    scale = got[:, 2 * width : 2 * width + 1].astype(f32)
    mine = lax.dynamic_slice_in_dim(pair, me_g * half, half, axis=2)
    blocks = pair.reshape(rows, 2, rep, grp, owner)
    blocks = lax.dynamic_index_in_dim(blocks, me_g, axis=3, keepdims=False)
    blocks = jnp.transpose(blocks, (2, 0, 1, 3)).reshape(rep, rows, 2 * owner)
    cols = lax.all_to_all(blocks, "rep", split_axis=0, concat_axis=0, tiled=True)
    cols = cols.reshape(rep * rows, 2, owner)
    w = jnp.transpose(weights, (1, 0, 2))
    pre = jnp.concatenate(
        [
            jnp.dot(mine[:, 0], w[0], preferred_element_type=f32),
            jnp.dot(mine[:, 0], w[1], preferred_element_type=f32),
            jnp.dot(mine[:, 1], w[2], preferred_element_type=f32),
        ],
        axis=1,
    )
    pre = lax.psum(pre, "grp")
    a, b, back = pre[:, :hid], pre[:, hid : 2 * hid], pre[:, 2 * hid :]
    sig = jax.nn.sigmoid(a)
    act = a * sig
    h = act * b
    dh = scale * back
    da = (dh * b * sig * (1.0 + a * (1.0 - sig))).astype(bf16)
    db = (dh * act).astype(bf16)
    hc = (scale * h).astype(bf16)
    pc = jnp.sum(h * back, axis=1, keepdims=True).astype(bf16)
    hidden = lax.all_gather(jnp.concatenate([da, db, hc], axis=1), "rep", axis=0, tiled=True)
    dn = (((1,), (1,)), ((), ()))
    px = lax.dot_general(da, w[0], dn, preferred_element_type=f32)
    px = (px + lax.dot_general(db, w[1], dn, preferred_element_type=f32)).astype(bf16)
    out = jnp.concatenate([px, jnp.broadcast_to(pc, (rows, pad))], axis=1)
    ret = lax.all_to_all(out, ("grp", "ep"), split_axis=0, concat_axis=0, tiled=True)
    ret = ret.reshape(grp, ep, CAP, half + pad).astype(f32)
    summed = jnp.sum(ret, axis=1)
    summed_x = jnp.transpose(summed[:, :, :half], (1, 0, 2)).reshape(CAP, width)
    summed_c = summed[0, :, half]
    highest = lax.Precision.HIGHEST
    tn = (((0,), (0,)), ((), ()))
    grad_tokens = lax.dot_general(slot_map, summed_x, tn, precision=highest).astype(bf16)
    per_token = jnp.sum(slot_map * summed_c[:, None], axis=0)
    grad_combine = match * per_token[:, None]
    gw = [
        lax.dot_general(cols[:, i], hidden[:, k * hid : (k + 1) * hid], tn, preferred_element_type=f32)
        for k, i in ((0, 0), (1, 0), (2, 1))
    ]
    return grad_tokens, grad_combine, jnp.stack(gw, axis=1)


def solution(mesh):
    split = P(("rep", "ep", "grp"), None)
    in_specs = (split, split, split, split, P("grp", None, "ep"))
    out_specs = (split, split, P(("rep", "grp"), None, "ep"))
    return jax.shard_map(local, mesh=mesh, in_specs=in_specs, out_specs=out_specs, check_vma=False)
```

time: 397 us -> 133 us (0.34)
  waiting for transfers between devices: 304 us -> 40.2 us
  blocking collectives: 16.6 us -> 40 us
  starting transfers between devices: 22.9 us -> 4.95 us
    all_gather x1, waiting for transfers between devices: 215 us -> 0.01 us  [local(): lax.all_gather(jnp.concatenate([da, db, hc], axis=1), 'rep', axis=0, tile...]
    reduce_scatter x1 -> x0, waiting for transfers between devices: 58.8 us -> none  [local(): lax.psum_scatter(jnp.concatenate([gate_up_term, down_term[:, None, :]], a...]
    psum x0 -> x1, waiting for transfers between devices: none -> 33.3 us  [local(): pre = lax.psum(pre, 'grp')]
    all_gather x1, blocking collectives: 6.61 us -> 32.9 us  [local(): got = lax.all_gather(sent, ('grp', 'ep'), axis=0, tiled=True)]
    all_to_all x6 -> x1, waiting for transfers between devices: 29.7 us -> 6.87 us  [local(): lax.all_to_all(out, ('grp', 'ep'), split_axis=0, concat_axis=0, tiled=True)]
    all_to_all x6 -> x1, starting transfers between devices: 22.8 us -> 4.87 us  [local(): lax.all_to_all(out, ('grp', 'ep'), split_axis=0, concat_axis=0, tiled=True)]
    dot_general x10 -> x11, matrix products: 23.4 us -> 22.3 us  [the longest x3 4.31 us: local(): lax.dot_general(cols[:, i], hidden[:, k * hid:(k + 1) * hid], tn, preferr...]
  transfers between devices with their start and end apart: 8 -> 3, of which waited for: 8 -> 2; matrix products, arithmetic and copies ran while one was open for 4% -> 8% of each run, Pallas kernels for 0% -> 0%
where the time goes in v1:
time: 133 us; the launch traced here: 132 us
  waiting for transfers between devices  40.2 us (30%)
  blocking collectives  40 us (30%)
  matrix products  22.3 us (17%)
  between operations  14.2 us (11%)
  other arithmetic  7.88 us (6%)
  starting transfers between devices  4.95 us (4%)
  local copies, waits for them, and re-layouts  2.39 us (2%)
    psum x1, waiting for transfers between devices, local(): pre = lax.psum(pre, 'grp')  33.3 us
    all_gather x1, blocking collectives, local(): got = lax.all_gather(sent, ('grp', 'ep'), axis=0, tiled=True)  32.9 us
    all_to_all x1, blocking collectives, local(): lax.all_to_all(blocks, 'rep', split_axis=0, concat_axis=0, tiled=True)  7.14 us
    all_to_all x1, waiting for transfers between devices, local(): lax.all_to_all(out, ('grp', 'ep'), split_axis=0, concat_axis=0, tiled=True)  6.87 us
    all_to_all x1, starting transfers between devices, local(): lax.all_to_all(out, ('grp', 'ep'), split_axis=0, concat_axis=0, tiled=True)  4.87 us
    dot_general x3, matrix products, local(): lax.dot_general(cols[:, i], hidden[:, k * hid:(k + 1) * hid], tn, preferr...  4.31 us
    dot_general x1, matrix products, local(): lax.dot_general(db, w[1], dn, preferred_element_type=f32)  3.24 us
    dot_general x1, matrix products, local(): px = lax.dot_general(da, w[0], dn, preferred_element_type=f32)  3.21 us
  transfers between devices with their start and end apart: 3, of which 2 were waited for; matrix products, arithmetic and copies ran while one was open for 8% of the time, Pallas kernels for 0%

profile of v1, /device:TPU:0, one launch (start us, length us, event | category | flops | bytes accessed | tf_op | source)
XLA Modules:
  0.0 131.9 jit_solution(17238979611261452542)
XLA Ops:
  7.2 0.7 convert_reduce_fusion.2
  8.0 0.1 copy.35
  8.1 0.2 reduce-window.8
  8.4 0.1 fusion.18
  8.5 0.2 convolution_convert_fusion.1
  8.7 1.2 convolution_convert_fusion.2
  10.0 32.9 %all-gather = bf16[8,4,4224]{2,1,0:T(4,128)(2,1)S(1)} all-gather(bf16[1,4,4224]{2,1,0:T(4,128)(2,1)S(1)} %maximum_bitcast_fusion), channel_id=1, replica_groups=mesh['rep'=4,'ep'=4,'grp'=2] {'grp','ep'}, dimensions={0}, use_global_device_ids=true | all-gather | bytes 304128 | tf_op jit(solution)/shard_map/all_gather | solution.py:37
  43.0 0.2 reshape.66
  43.2 0.3 constant_dynamic-slice_fusion
  43.5 2.7 %fusion.2 = f32[32,1792]{1,0:T(8,128)S(1)} fusion(bf16[3,1024,1792]{2,1,0:T(8,128)(2,1)} %bitcast.58, bf16[32,1,1024]{2,1,0:T(2,128)(2,1)S(1)} %get-tuple-element.9), kind=kOutput, calls=%fused_computation.6 | convolution fusion | flops 117440512 | bytes 3964928 | tf_op jit(solution)/shard_map/dot_general | solution.py:49
  46.3 2.7 %fusion.4 = f32[32,1792]{1,0:T(8,128)S(1)} fusion(bf16[3,1024,1792]{2,1,0:T(8,128)(2,1)} %bitcast.59, bf16[32,1,1024]{2,1,0:T(2,128)(2,1)S(1)} %get-tuple-element.9), kind=kOutput, calls=%fused_computation.8 | convolution fusion | flops 117440512 | bytes 3964928 | tf_op jit(solution)/shard_map/dot_general | solution.py:50
  49.0 2.8 %fusion = f32[32,1792]{1,0:T(8,128)S(1)} fusion(bf16[3,1024,1792]{2,1,0:T(8,128)(2,1)} %bitcast.60, bf16[32,1,1024]{2,1,0:T(2,128)(2,1)S(1)} %get-tuple-element.10), kind=kOutput, calls=%fused_computation.2 | convolution fusion | flops 117440512 | bytes 3964928 | tf_op jit(solution)/shard_map/dot_general | solution.py:51
  51.8 0.9 pad_maximum_fusion.1
  52.7 0.2 reshape_reshape.3
  53.0 33.3 %all-reduce.2.cloned.1.call-done = f32[32,5376]{1,0:T(8,128)} async-done(((f32[32,5376]{1,0:T(8,128)}), f32[32,5376]{1,0:T(8,128)}) %all-reduce.2.cloned.1.call-update) | async-done | bytes 688144 | tf_op jit(solution)/shard_map/psum | solution.py:55
  86.3 1.4 %multiply_convert_fusion = (bf16[32,1792]{1,0:T(8,128)(2,1)S(1)}, bf16[32,1792]{1,0:T(8,128)(2,1)S(1)}, bf16[32,1792]{1,0:T(8,128)(2,1)S(1)}, bf16[32]{0:T(256)(128)(2,1)S(1)}) fusion(f32[32]{0:T(128)S(1)} %convert_reduce_fusion.1, f32[32,5376]{1,0:T(8,128)} %all-reduce.2.cloned.1.call-done), kind=kLoop, calls=%fused_computation.22 | loop fusion | flops 1089504 | bytes 1032384 | tf_op jit(solution)/shard_map/convert_element_type | solution.py:63
  87.7 0.8 pad_maximum_fusion.2
  88.5 0.3 constant_dynamic-slice_fusion.1
  88.9 7.1 %all_to_all.14 = bf16[4,32,512]{2,1,0:T(8,128)(2,1)S(1)} all-to-all(bf16[4,32,512]{2,1,0:T(8,128)(2,1)S(1)} %bitcast.64), channel_id=1, replica_groups=mesh['rep'=4,'ep'=4,'grp'=2] {'rep'}, dimensions={0} | all-to-all | bytes 262144 | tf_op jit(solution)/shard_map/all_to_all | solution.py:44
  96.1 3.2 %fusion.1 = f32[32,1024]{1,0:T(8,128)S(1)} fusion(bf16[32,1792]{1,0:T(8,128)(2,1)S(1)} %get-tuple-element.7, bf16[3,1024,1792]{2,1,0:T(8,128)(2,1)} %bitcast.61), kind=kOutput, calls=%fused_computation.5 | convolution fusion | flops 117440512 | bytes 3915776 | tf_op jit(solution)/shard_map/dot_general | solution.py:67
  99.3 3.2 %fusion.6 = bf16[32,1024]{1,0:T(8,128)(2,1)S(1)} fusion(f32[32,1024]{1,0:T(8,128)S(1)} %fusion.1, bf16[32,1792]{1,0:T(8,128)(2,1)S(1)} %get-tuple-element.6, bf16[3,1024,1792]{2,1,0:T(8,128)(2,1)} %bitcast.62), kind=kOutput, calls=%fused_computation.16 | convolution fusion | flops 117506048 | bytes 3981312 | tf_op jit(solution)/shard_map/dot_general | solution.py:68
  102.7 0.7 all_to_all.9
  103.3 4.9 %all-to-all-start = ((bf16[8,4,1152]{2,1,0:T(4,128)(2,1)}), bf16[8,4,1152]{2,1,0:T(4,128)(2,1)S(1)}, u32[]{:S(2)}, u32[]{:S(2)}) async-start(bf16[8,4,1152]{2,1,0:T(4,128)(2,1)} %all_to_all.9), calls=%async_computation | async-start | bytes 147456 | tf_op jit(solution)/shard_map/all_to_all | solution.py:70
  108.2 0.2 fusion.32
  108.4 6.9 %all-to-all-done = bf16[8,4,1152]{2,1,0:T(4,128)(2,1)S(1)} async-done(((bf16[8,4,1152]{2,1,0:T(4,128)(2,1)}), bf16[8,4,1152]{2,1,0:T(4,128)(2,1)S(1)}, u32[]{:S(2)}, u32[]{:S(2)}) %all-to-all-start) | async-done | bytes 73760 | tf_op jit(solution)/shard_map/all_to_all | solution.py:70
  115.3 0.1 slice_reduce_fusion
  115.5 0.6 broadcast_select_fusion
  116.1 1.8 %convolution_convert_fusion = bf16[128,2048]{1,0:T(8,128)(2,1)} fusion(f32[4,2048]{1,0:T(4,128)S(1)} %bitcast.65, f32[128]{0:T(128)S(1)} %get-tuple-element.3, f32[128]{0:T(128)S(1)} %sub.10), kind=kOutput, calls=%fused_computation.12 | convolution fusion | flops 12846080 | bytes 558080 | tf_op jit(solution)/shard_map/dot_general | solution.py:77
  117.9 1.4 %convolution_bitcast_fusion.1 = f32[256,1,1792]{2,0,1:T(8,128)S(1)} fusion(bf16[128,5376]{1,0:T(8,128)(2,1)} %all-gather.3.cloned.1.call-done, bf16[128,1,256]{2,1,0:T(2,128)(2,1)S(1)} %get-tuple-element.11), kind=kOutput, calls=%fused_computation.10 | convolution fusion | flops 117440512 | bytes 2359296 | tf_op jit(solution)/shard_map/dot_general | solution.py:81
  119.4 1.4 %convolution_bitcast_fusion.2 = f32[256,1,1792]{2,0,1:T(8,128)S(1)} fusion(bf16[128,5376]{1,0:T(8,128)(2,1)} %all-gather.3.cloned.1.call-done, bf16[128,1,256]{2,1,0:T(2,128)(2,1)S(1)} %get-tuple-element.11), kind=kOutput, calls=%fused_computation.11 | convolution fusion | flops 117440512 | bytes 2359296 | tf_op jit(solution)/shard_map/dot_general | solution.py:81
  120.8 1.4 %convolution_bitcast_fusion = f32[256,1,1792]{2,0,1:T(8,128)S(1)} fusion(bf16[128,5376]{1,0:T(8,128)(2,1)} %all-gather.3.cloned.1.call-done, bf16[128,1,256]{2,1,0:T(2,128)(2,1)S(1)} %get-tuple-element.12), kind=kOutput, calls=%fused_computation.9 | convolution fusion | flops 117440512 | bytes 2359296 | tf_op jit(solution)/shard_map/dot_general | solution.py:81
  122.2 2.8 %pad_maximum_fusion = f32[256,3,1792]{2,0,1:T(8,128)} fusion(f32[256,1,1792]{2,0,1:T(8,128)S(1)} %convolution_bitcast_fusion, f32[256,1,1792]{2,0,1:T(8,128)S(1)} %convolution_bitcast_fusion.1, f32[256,1,1792]{2,0,1:T(8,128)S(1)} %convolution_bitcast_fusion.2), kind=kLoop, calls=%fused_computation | loop fusion | flops 2752512 | bytes 11010048 | tf_op jit(solution)/shard_map/stack | solution.py:84
  (24 shorter events, 0.9 us)
Async XLA Ops:
  7.2 1.3 %copy-start = (bf16[128,2048]{1,0:T(8,128)(2,1)S(1)}, bf16[128,2048]{1,0:T(8,128)(2,1)}, u32[]{:S(2)}) copy-start(bf16[128,2048]{1,0:T(8,128)(2,1)} %param.6) | copy-start | bytes 1572868
  7.2 79.1 %all-reduce.2.cloned.1.call-start = ((), (), s32[]{:S(2)}) async-start(), calls=%async_computation.2 | async-start | bytes 1376256 | tf_op jit(solution)/shard_map/psum | solution.py:55
  52.7 65.2 %all-gather.3.cloned.1.call-start = ((), (), s32[]{:S(2)}) async-start(), calls=%async_computation.3 | async-start | bytes 1720320 | tf_op jit(solution)/shard_map/all_gather | solution.py:65
  96.1 19.4 %copy-start.1 = (s32[128,2]{0,1:T(2,128)S(1)}, s32[128,2]{0,1:T(2,128)}, u32[]{:S(2)}) copy-start(s32[128,2]{0,1:T(2,128)} %param.7) | copy-start | bytes 3076
  103.3 11.9 %all-to-all-start = ((bf16[8,4,1152]{2,1,0:T(4,128)(2,1)}), bf16[8,4,1152]{2,1,0:T(4,128)(2,1)S(1)}, u32[]{:S(2)}, u32[]{:S(2)}) async-start(bf16[8,4,1152]{2,1,0:T(4,128)(2,1)} %all_to_all.9), calls=%async_computation | async-start | bytes 147456 | tf_op jit(solution)/shard_map/all_to_all | solution.py:70
Sparse Core Ops, SparseCore 0:
  52.8 33.4 all-reduce.1
  88.7 18.5 all-gather.2

commit v2 on v1

--- a/solution.py
+++ b/solution.py
@@ -1,6 +1,10 @@
+import functools
+
 import jax
 import jax.numpy as jnp
 from jax import lax
+from jax.experimental import pallas as pl
+from jax.experimental.pallas import tpu as pltpu
 from jax.sharding import PartitionSpec as P
 
 FLIGHT = 1
@@ -83,9 +87,309 @@
     ]
     return grad_tokens, grad_combine, jnp.stack(gw, axis=1)
 
+CHUNK = 256
+MESH = pl.DeviceIdType.MESH
+F32, BF16 = jnp.float32, jnp.bfloat16
+
+
+def pick(sources, piece, flip=False):
+    shape = (sources * 16, sources * CAP) if flip else (sources * CAP, sources * 16)
+    row = lax.broadcasted_iota(jnp.int32, shape, 1 if flip else 0)
+    col = lax.broadcasted_iota(jnp.int32, shape, 0 if flip else 1)
+    return (col == (row >> 2) * 16 + piece * CAP + (row & 3)).astype(F32).astype(BF16)
+
+
+def mm(a, b):
+    return jnp.dot(a, b, preferred_element_type=F32)
+
+
+def mm_nt(a, b):
+    return lax.dot_general(a, b, (((1,), (1,)), ((), ())), preferred_element_type=F32)
+
+
+def exchange_kernel(
+    dims, slots_ref, comb_ref, tok_ref, gout_ref, w_hbm, hid_ref, cols_ref, sum_ref,
+    w_ref, sent, sent2, got, got2, part, psend, precv, back_s, back_r, acc,
+    w_sem, g_sem, g2_sem, y_sem, x_sem, c_sem, f_sem, xc_sem, b_sem,
+):
+    rep, ep, grp, half, owner, hid = dims
+    peers, rows, nch = ep * grp, ep * grp * CAP, hid // CHUNK
+    hw, ow, qw = half // 2, owner // 2, half // 4
+    r, j, g = lax.axis_index("rep"), lax.axis_index("ep"), lax.axis_index("grp")
+    me = g * ep + j
+
+    def peer(d):
+        other = lax.rem(me + d, peers)
+        return other, {"ep": lax.rem(other, ep), "grp": lax.div(other, ep)}
+
+    def rep_peer(d):
+        return lax.rem(r + d, rep)
+
+    barrier = pltpu.get_barrier_semaphore()
+    for d in range(1, peers):
+        pl.semaphore_signal(barrier, inc=1, device_id=peer(d)[1], device_id_type=MESH)
+    for d in range(1, rep):
+        pl.semaphore_signal(barrier, inc=1, device_id={"rep": rep_peer(d)}, device_id_type=MESH)
+    loads = [pltpu.make_async_copy(w_hbm.at[k], w_ref.at[k], w_sem.at[k]) for k in range(3)]
+    for load in loads:
+        load.start()
+
+    srcs = (tok_ref, gout_ref)
+    for gg in range(grp):
+        total = jnp.zeros((16, hw), F32)
+        for lohi in range(2):
+            for xy in range(2):
+                at = (gg * 2 + lohi) * hw
+                total += mm(slots_ref[lohi * 2 + xy], srcs[xy][:, at : at + hw])
+        sent[gg, :, 0:hw] = total.astype(BF16)
+        sent[gg, :, hw : hw + 128] = mm(slots_ref[0], comb_ref[...]).astype(BF16)
+    for gg in range(grp):
+        for rr in range(rep):
+            total = jnp.zeros((16, ow), F32)
+            for lohi in range(2):
+                for xy in range(2):
+                    at = (rr * grp + gg) * owner + lohi * ow
+                    total += mm(slots_ref[lohi * 2 + xy], srcs[xy][:, at : at + ow])
+            sent2[gg, rr] = total.astype(BF16)
+    pl.semaphore_wait(barrier, peers - 1 + rep - 1)
+
+    gather, gather2 = [], []
+    for out, src, dst, sem in ((gather, sent, got, g_sem), (gather2, sent2, got2, g2_sem)):
+        for d in range(1, peers):
+            other, where = peer(d)
+            copy = pltpu.make_async_remote_copy(
+                src_ref=src.at[lax.div(other, ep)], dst_ref=dst.at[me],
+                send_sem=sem.at[0, d], recv_sem=sem.at[1, d],
+                device_id=where, device_id_type=MESH,
+            )
+            copy.start()
+            out.append(copy)
+    got[me] = sent[g]
+    got2[me] = sent2[g]
+    for copy in gather:
+        copy.wait_recv()
+    flat = got[...].reshape(peers * 16, hw + 128)
+    body = flat[:, :hw]
+    x = jnp.concatenate([mm(pick(peers, 0), body), mm(pick(peers, 2), body)], axis=1).astype(BF16)
+    y = jnp.concatenate([mm(pick(peers, 1), body), mm(pick(peers, 3), body)], axis=1).astype(BF16)
+    scale = mm(pick(peers, 0), flat[:, hw:])[:, :1]
+    for load in loads:
+        load.wait()
+
+    def across(c):
+        return pltpu.make_async_remote_copy(
+            src_ref=psend.at[c], dst_ref=precv.at[c],
+            send_sem=y_sem.at[0, c], recv_sem=y_sem.at[1, c],
+            device_id={"grp": 1 - g}, device_id_type=MESH,
+        )
+
+    def spread(c, who, sem, to):
+        return pltpu.make_async_remote_copy(
+            src_ref=hid_ref.at[who, c], dst_ref=hid_ref.at[who, c],
+            send_sem=sem.at[0, c], recv_sem=sem.at[1, c],
+            device_id={"rep": to}, device_id_type=MESH,
+        )
+
+    far, near = lax.rem(r + 2, rep), r + 1 - 2 * lax.rem(r, 2)
+
+    @pl.loop(0, nch)
+    def _(c):
+        at = pl.ds(pl.multiple_of(c * CHUNK, CHUNK), CHUNK)
+        for k in range(3):
+            value = mm(y if k == 2 else x, w_ref[k, :, at])
+            small = value.astype(BF16)
+            part[c, k] = value
+            psend[c, k] = small
+        across(c).start()
+
+    for copy in gather2:
+        copy.wait_recv()
+    moves = []
+    for d in range(1, rep):
+        to = rep_peer(d)
+        copy = pltpu.make_async_remote_copy(
+            src_ref=got2.at[:, to], dst_ref=cols_ref.at[r],
+            send_sem=xc_sem.at[0, d], recv_sem=xc_sem.at[1, d],
+            device_id={"rep": to}, device_id_type=MESH,
+        )
+        copy.start()
+        moves.append(copy)
+    for p in range(peers):
+        cols_ref[r, p] = got2[p, r]
+    acc[...] = jnp.zeros_like(acc)
+
+    def step(c, sums):
+        at = pl.ds(pl.multiple_of(c * CHUNK, CHUNK), CHUNK)
+        across(c).wait_recv()
+        own = [part[c, k] for k in range(3)]
+        a, b, bk = [own[k] + precv[c, k].astype(F32) for k in range(3)]
+        lost_a, lost_b, lost_bk = [own[k] - psend[c, k].astype(F32) for k in range(3)]
+        sig = jax.nn.sigmoid(a)
+        act = a * sig
+        h = act * b
+        slope_a = bk * b * sig * (1.0 + a * (1.0 - sig))
+        slope_b = bk * act
+        da = (scale * slope_a).astype(BF16)
+        db = (scale * slope_b).astype(BF16)
+        hid_ref[r, c, 0] = da
+        hid_ref[r, c, 1] = db
+        hid_ref[r, c, 2] = (scale * h).astype(BF16)
+        spread(c, r, x_sem, far).start()
+        spread(c, r, c_sem, near).start()
+        acc[...] += mm_nt(da, w_ref[0, :, at]) + mm_nt(db, w_ref[1, :, at])
+
+        @pl.when(c > 0)
+        def _():
+            spread(c - 1, far, x_sem, far).wait_recv()
+            spread(c - 1, far, f_sem, near).start()
+
+        fix = slope_a * lost_a + slope_b * lost_b + h * lost_bk
+        return sums[0] + h * bk, sums[1] + fix
+
+    wide = jnp.zeros((rows, CHUNK), F32)
+    sums = lax.fori_loop(0, nch, step, (wide, wide))
+    pc, fix = [jnp.sum(v, axis=1, keepdims=True) for v in sums]
+    px = acc[...].astype(BF16)
+    pcb = jnp.broadcast_to(pc, (rows, 128)).astype(BF16)
+    fixb = jnp.broadcast_to(fix, (rows, 128)).astype(BF16)
+    total = jnp.zeros((peers * 16, qw), F32)
+    for q in range(4):
+        total += mm(pick(peers, q, True), px[:, q * qw : (q + 1) * qw])
+    back_s[:, :, 0:qw] = total.astype(BF16).reshape(peers, 16, qw)
+    extra = mm(pick(peers, 0, True), pcb) + mm(pick(peers, 1, True), fixb)
+    back_s[:, :, qw : qw + 128] = extra.astype(BF16).reshape(peers, 16, 128)
+    returns = []
+    for d in range(1, peers):
+        other, where = peer(d)
+        copy = pltpu.make_async_remote_copy(
+            src_ref=back_s.at[other], dst_ref=back_r.at[me],
+            send_sem=b_sem.at[0, d], recv_sem=b_sem.at[1, d],
+            device_id=where, device_id_type=MESH,
+        )
+        copy.start()
+        returns.append(copy)
+    back_r[me] = back_s[me]
+    spread(nch - 1, far, x_sem, far).wait_recv()
+    spread(nch - 1, far, f_sem, near).start()
+    for copy in returns:
+        copy.wait_recv()
+    for gg in range(grp):
+        total = back_r[gg * ep].astype(F32)
+        for jj in range(1, ep):
+            total += back_r[gg * ep + jj].astype(F32)
+        sum_ref[gg] = total
+
+    for copy in gather + gather2 + returns:
+        copy.wait_send()
+    for copy in moves:
+        copy.wait()
+
+    @pl.loop(0, nch)
+    def _(c):
+        across(c).wait_send()
+        spread(c, r, x_sem, far).wait_send()
+        spread(c, r, c_sem, near).wait()
+        spread(c, far, f_sem, near).wait()
+
+
+def contract_kernel(cols_ref, hid_ref, sum_ref, slots_ref, gw_ref, gt_ref, xt):
+    blocks, ow = cols_ref.shape[0] // 16, cols_ref.shape[1]
+
+    @pl.when(pl.program_id(0) == 0)
+    def _():
+        for xy in range(2):
+            both = [mm(pick(blocks, lohi * 2 + xy), cols_ref[...]) for lohi in range(2)]
+            xt[xy] = jnp.concatenate(both, axis=1).T.astype(BF16)
+        qw = sum_ref.shape[2] - 128
+        for gg in range(sum_ref.shape[0]):
+            rows = sum_ref[gg, :, 0:qw].astype(BF16)
+            for q in range(4):
+                at = (gg * 4 + q) * qw
+                gt_ref[:, at : at + qw] = lax.dot_general(
+                    slots_ref[q], rows, (((0,), (0,)), ((), ())), preferred_element_type=F32
+                ).astype(BF16)
+
+    for k in range(3):
+        h = hid_ref[:, pl.program_id(0), k].reshape(-1, hid_ref.shape[4])
+        gw_ref[k] = mm(xt[k // 2], h)
+
+
+def direct(tokens, grad_out, expert_ids, combine, weights):
+    ep, rep, grp = lax.axis_size("ep"), lax.axis_size("rep"), lax.axis_size("grp")
+    count, width = tokens.shape
+    half, owner, hid = width // grp, width // (rep * grp), weights.shape[2]
+    peers, rows, nch = ep * grp, ep * grp * CAP, hid // CHUNK
+    hw, ow, qw = half // 2, owner // 2, half // 4
+    match, combined, slot_map = route_slots(expert_ids, combine)
+    slots = jnp.stack([jnp.pad(slot_map, ((q * CAP, 12 - q * CAP), (0, 0))) for q in range(4)]).astype(BF16)
+    comb = jnp.broadcast_to(combined[:, None], (count, 128)).astype(BF16)
+    vmem = pl.BlockSpec(memory_space=pltpu.VMEM)
+    dma = pltpu.SemaphoreType.DMA
+    hidden, cols, sums = pl.pallas_call(
+        functools.partial(exchange_kernel, (rep, ep, grp, half, owner, hid)),
+        out_shape=(
+            jax.ShapeDtypeStruct((rep, nch, 3, rows, CHUNK), BF16),
+            jax.ShapeDtypeStruct((rep, peers, 16, ow), BF16),
+            jax.ShapeDtypeStruct((grp, 16, qw + 128), F32),
+        ),
+        in_specs=[vmem] * 4 + [pl.BlockSpec(memory_space=pltpu.HBM)],
+        out_specs=(vmem, vmem, vmem),
+        scratch_shapes=[
+            pltpu.VMEM((3, half, hid), BF16),
+            pltpu.VMEM((grp, 16, hw + 128), BF16),
+            pltpu.VMEM((grp, rep, 16, ow), BF16),
+            pltpu.VMEM((peers, 16, hw + 128), BF16),
+            pltpu.VMEM((peers, rep, 16, ow), BF16),
+            pltpu.VMEM((nch, 3, rows, CHUNK), F32),
+            pltpu.VMEM((nch, 3, rows, CHUNK), BF16),
+            pltpu.VMEM((nch, 3, rows, CHUNK), BF16),
+            pltpu.VMEM((peers, 16, qw + 128), BF16),
+            pltpu.VMEM((peers, 16, qw + 128), BF16),
+            pltpu.VMEM((rows, half), F32),
+            dma((3,)),
+            dma((2, peers)),
+            dma((2, peers)),
+            dma((2, nch)),
+            dma((2, nch)),
+            dma((2, nch)),
+            dma((2, nch)),
+            dma((2, rep)),
+            dma((2, peers)),
+        ],
+        compiler_params=pltpu.CompilerParams(
+            collective_id=0, has_side_effects=True, vmem_limit_bytes=40 << 20
+        ),
+    )(slots, comb, tokens, grad_out, jnp.transpose(weights, (1, 0, 2)))
+    gw, grad_tokens = pl.pallas_call(
+        contract_kernel,
+        grid=(nch,),
+        out_shape=(
+            jax.ShapeDtypeStruct((3, owner, hid), F32),
+            jax.ShapeDtypeStruct((count, width), BF16),
+        ),
+        in_specs=[vmem] * 4,
+        out_specs=(
+            pl.BlockSpec((3, owner, CHUNK), lambda c: (0, 0, c)),
+            pl.BlockSpec((count, width), lambda c: (0, 0)),
+        ),
+        scratch_shapes=[pltpu.VMEM((2, owner, rep * rows), BF16)],
+    )(cols.reshape(rep * peers * 16, ow), hidden, sums, slots)
+    combine_sum = sums[0, :CAP, qw] + sums[1, CAP : 2 * CAP, qw]
+    per_token = jnp.sum(slot_map * combine_sum[:, None], axis=0)
+    return grad_tokens, match * per_token[:, None], jnp.transpose(gw, (1, 0, 2))
+
 
 def solution(mesh):
     split = P(("rep", "ep", "grp"), None)
     in_specs = (split, split, split, split, P("grp", None, "ep"))
     out_specs = (split, split, P(("rep", "grp"), None, "ep"))
-    return jax.shard_map(local, mesh=mesh, in_specs=in_specs, out_specs=out_specs, check_vma=False)
+    sizes = dict(mesh.shape)
+
+    def body(tokens, grad_out, expert_ids, combine, weights):
+        owner = tokens.shape[1] // (sizes["rep"] * sizes["grp"])
+        small = sizes["rep"] == 4 and sizes["grp"] == 2 and sizes["ep"] <= 8
+        fits = owner % 256 == 0 and weights.shape[2] % CHUNK == 0
+        run = direct if small and fits else local
+        return run(tokens, grad_out, expert_ids, combine, weights)
+
+    return jax.shard_map(body, mesh=mesh, in_specs=in_specs, out_specs=out_specs, check_vma=False)

time: 133 us -> 50.9 us (0.38)
  waiting for transfers between devices: 40.2 us -> 0 us
  Pallas kernels: 0 us -> 40 us
  blocking collectives: 40 us -> 0 us
  matrix products: 22.3 us -> 0 us
  between operations: 14.2 us -> 0.71 us
  other arithmetic: 7.88 us -> 1.78 us
  local copies, waits for them, and re-layouts: 2.39 us -> 8.15 us
  starting transfers between devices: 4.95 us -> 0 us
    pallas_call x0 -> x2, Pallas kernels: none -> 40 us  [the longest x1 33.7 us: direct(): pl.pallas_call(functools.partial(exchange_kernel, (rep, ep, grp, half, ow...]
    psum x1 -> x0, waiting for transfers between devices: 33.3 us -> none  [local(): pre = lax.psum(pre, 'grp')]
    all_gather x1 -> x0, blocking collectives: 32.9 us -> none  [local(): got = lax.all_gather(sent, ('grp', 'ep'), axis=0, tiled=True)]
    dot_general x11 -> x0, matrix products: 22.3 us -> none  [the longest x3 4.31 us: local(): lax.dot_general(cols[:, i], hidden[:, k * hid:(k + 1) * hid], tn, preferr...]
    unnamed x5 -> x16, local copies, waits for them, and re-layouts: 0.08 us -> 7.94 us
    all_to_all x1 -> x0, blocking collectives: 7.14 us -> none  [local(): lax.all_to_all(blocks, 'rep', split_axis=0, concat_axis=0, tiled=True)]
    all_to_all x1 -> x0, waiting for transfers between devices: 6.87 us -> none  [local(): lax.all_to_all(out, ('grp', 'ep'), split_axis=0, concat_axis=0, tiled=True)]
    all_to_all x1 -> x0, starting transfers between devices: 4.87 us -> none  [local(): lax.all_to_all(out, ('grp', 'ep'), split_axis=0, concat_axis=0, tiled=True)]
  transfers between devices with their start and end apart: 3 -> 0, of which waited for: 2 -> 0; matrix products, arithmetic and copies ran while one was open for 8% -> 0% of each run, Pallas kernels for 0% -> 0%
where the time goes in v2:
time: 50.9 us; the launch traced here: 50.6 us
  Pallas kernels  40 us (79%)
  local copies, waits for them, and re-layouts  8.15 us (16%)
  other arithmetic  1.78 us (3%)
  between operations  0.71 us (1%)
    pallas_call x1, Pallas kernels, direct(): pl.pallas_call(functools.partial(exchange_kernel, (rep, ep, grp, half, ow...  33.7 us
    unnamed x16, local copies, waits for them, and re-layouts  7.94 us
    pallas_call x1, Pallas kernels, direct(): pl.pallas_call(contract_kernel, grid=(nch,), out_shape=(jax.ShapeDtypeStr...  6.27 us

profile of v2, /device:TPU:0, one launch (start us, length us, event | category | flops | bytes accessed | tf_op | source)
XLA Modules:
  0.0 50.6 jit_solution(6166298072284781742)
XLA Ops:
  0.6 0.7 %select_reduce_fusion = (bf16[128]{0:T(256)(128)(2,1)S(1)}, f32[128]{0:T(128)S(1)}) fusion(bf16[128,2]{0,1:T(2,128)(2,1)} %param.8, s32[128,2]{0,1:T(2,128)} %param.7), kind=kLoop, calls=%fused_computation.10 | loop fusion | flops 1280 | bytes 2304 | tf_op jit(solution)/shard_map/reduce_sum | solution.py:17
  1.3 0.1 broadcast_in_dim.2.comb_ref
  1.4 0.1 copy.9
  1.5 0.2 reduce-window.8
  1.7 0.1 reduce
  1.9 0.0 copy-start
  1.9 4.1 %copy-done = bf16[1024,3,1792]{2,0,1:T(8,128)(2,1)S(1)} copy-done((bf16[1024,3,1792]{2,0,1:T(8,128)(2,1)S(1)}, bf16[1024,3,1792]{2,0,1:T(8,128)(2,1)}, u32[]{:S(2)}) %copy-start) | copy-done | bytes 11010072
  6.0 0.0 copy-start.2
  6.0 1.0 %copy-done.2 = bf16[128,2048]{1,0:T(8,128)(2,1)S(1)} copy-done((bf16[128,2048]{1,0:T(8,128)(2,1)S(1)}, bf16[128,2048]{1,0:T(8,128)(2,1)}, u32[]{:S(2)}) %copy-start.2) | copy-done | bytes 524312
  7.1 0.0 copy-start.3
  7.1 1.0 %copy-done.3 = bf16[128,2048]{1,0:T(8,128)(2,1)S(1)} copy-done((bf16[128,2048]{1,0:T(8,128)(2,1)S(1)}, bf16[128,2048]{1,0:T(8,128)(2,1)}, u32[]{:S(2)}) %copy-start.3) | copy-done | bytes 524312
  8.1 0.0 copy-start.4
  8.1 0.0 copy-start.7
  8.1 33.7 %shard_map.76 = (bf16[4,7,3,32,256]{4,3,2,1,0:T(8,128)(2,1)S(1)}, bf16[4,8,16,128]{3,2,1,0:T(8,128)(2,1)S(1)}, f32[2,16,384]{2,1,0:T(8,128)S(1)}) custom-call(bf16[4,16,128]{2,1,0:T(8,128)(2,1)S(1)} %pad_maximum_fusion.slots_ref, bf16[128,128]{1,0:T(8,128)(2,1)S(1)} %broadcast_in_dim.2.comb_ref, bf16[128,2048]{1,0:T(8,128)(2,1)S(1)} %copy-done.2, ...), custom_call_target="tpu_custom_call" | custom-call | tf_op jit(solution)/shard_map/pallas_call | solution.py:328
  41.8 0.0 copy-done.4
  41.9 0.0 copy-start.1
  41.9 1.1 %copy-done.1 = bf16[4,7,3,32,256]{4,3,2,1,0:T(8,128)(2,1)} copy-done((bf16[4,7,3,32,256]{4,3,2,1,0:T(8,128)(2,1)}, bf16[4,7,3,32,256]{4,3,2,1,0:T(8,128)(2,1)S(1)}, u32[]{:S(2)}) %copy-start.1) | copy-done | bytes 1376280
  42.9 0.0 copy-start.5
  42.9 0.7 %copy-done.5 = bf16[4,8,16,128]{3,2,1,0:T(8,128)(2,1)} copy-done((bf16[4,8,16,128]{3,2,1,0:T(8,128)(2,1)}, bf16[4,8,16,128]{3,2,1,0:T(8,128)(2,1)S(1)}, u32[]{:S(2)}) %copy-start.5) | copy-done | bytes 131096
  43.6 0.0 copy-start.6
  43.6 0.1 add_reduce_fusion
  43.7 0.1 fusion
  43.8 0.0 copy-done.7
  43.8 0.6 %broadcast_select_fusion = f32[128,2]{0,1:T(2,128)} fusion(f32[128]{0:T(128)S(1)} %fusion, s32[128,2]{0,1:T(2,128)S(1)} %copy-done.7), kind=kLoop, calls=%fused_computation.12 | loop fusion | flops 512 | bytes 2560 | tf_op jit(solution)/shard_map/mul | solution.py:379
  44.4 0.0 copy-done.6
  44.4 6.3 %shard_map.77 = (f32[3,256,1792]{2,1,0:T(8,128)}, bf16[128,2048]{1,0:T(8,128)(2,1)}) custom-call(bf16[512,128]{1,0:T(8,128)(2,1)} %bitcast.13, bf16[4,7,3,32,256]{4,3,2,1,0:T(8,128)(2,1)} %copy-done.1, f32[2,16,384]{2,1,0:T(8,128)} %copy-done.6, bf16[4,16,128]{2,1,0:T(8,128)(2,1)} %copy-done.4), custom_call_target="tpu_custom_call" | custom-call | tf_op jit(solution)/shard_map/pallas_call | solution.py:363
  (4 shorter events, 0.0 us)
Async XLA Ops:
  1.9 4.1 %copy-start = (bf16[1024,3,1792]{2,0,1:T(8,128)(2,1)S(1)}, bf16[1024,3,1792]{2,0,1:T(8,128)(2,1)}, u32[]{:S(2)}) copy-start(bf16[1024,3,1792]{2,0,1:T(8,128)(2,1)} %param.9) | copy-start | bytes 33030148
  6.0 1.0 %copy-start.2 = (bf16[128,2048]{1,0:T(8,128)(2,1)S(1)}, bf16[128,2048]{1,0:T(8,128)(2,1)}, u32[]{:S(2)}) copy-start(bf16[128,2048]{1,0:T(8,128)(2,1)} %tok_ref.1) | copy-start | bytes 1572868
  7.1 1.0 %copy-start.3 = (bf16[128,2048]{1,0:T(8,128)(2,1)S(1)}, bf16[128,2048]{1,0:T(8,128)(2,1)}, u32[]{:S(2)}) copy-start(bf16[128,2048]{1,0:T(8,128)(2,1)} %gout_ref.1) | copy-start | bytes 1572868
  8.1 33.7 %copy-start.4 = (bf16[4,16,128]{2,1,0:T(8,128)(2,1)}, bf16[4,16,128]{2,1,0:T(8,128)(2,1)S(1)}, u32[]{:S(2)}) copy-start(bf16[4,16,128]{2,1,0:T(8,128)(2,1)S(1)} %pad_maximum_fusion.slots_ref) | copy-start | bytes 49156
  8.1 35.7 %copy-start.7 = (s32[128,2]{0,1:T(2,128)S(1)}, s32[128,2]{0,1:T(2,128)}, u32[]{:S(2)}) copy-start(s32[128,2]{0,1:T(2,128)} %param.7) | copy-start | bytes 3076
  41.9 1.1 %copy-start.1 = (bf16[4,7,3,32,256]{4,3,2,1,0:T(8,128)(2,1)}, bf16[4,7,3,32,256]{4,3,2,1,0:T(8,128)(2,1)S(1)}, u32[]{:S(2)}) copy-start(bf16[4,7,3,32,256]{4,3,2,1,0:T(8,128)(2,1)S(1)} %get-tuple-element.9.hid_ref) | copy-start | bytes 4128772
  42.9 0.7 %copy-start.5 = (bf16[4,8,16,128]{3,2,1,0:T(8,128)(2,1)}, bf16[4,8,16,128]{3,2,1,0:T(8,128)(2,1)S(1)}, u32[]{:S(2)}) copy-start(bf16[4,8,16,128]{3,2,1,0:T(8,128)(2,1)S(1)} %get-tuple-element.8) | copy-start | bytes 393220
  43.6 0.8 %copy-start.6 = (f32[2,16,384]{2,1,0:T(8,128)}, f32[2,16,384]{2,1,0:T(8,128)S(1)}, u32[]{:S(2)}) copy-start(f32[2,16,384]{2,1,0:T(8,128)S(1)} %get-tuple-element.10.sum_ref) | copy-start | bytes 147460

commit v3 on v2

--- a/solution.py
+++ b/solution.py
@@ -357,7 +357,7 @@
             dma((2, peers)),
         ],
         compiler_params=pltpu.CompilerParams(
-            collective_id=0, has_side_effects=True, vmem_limit_bytes=40 << 20
+            collective_id=0, has_side_effects=True, vmem_limit_bytes=60 << 20
         ),
     )(slots, comb, tokens, grad_out, jnp.transpose(weights, (1, 0, 2)))
     gw, grad_tokens = pl.pallas_call(

time: 50.9 us -> 47.2 us (0.927)
  local copies, waits for them, and re-layouts: 8.15 us -> 0.83 us
  Pallas kernels: 40 us -> 42.4 us
  other arithmetic: 1.78 us -> 3.06 us
    unnamed x16 -> x2, local copies, waits for them, and re-layouts: 7.94 us -> 0.01 us
    pallas_call x1, Pallas kernels: 33.7 us -> 36.1 us  [direct(): pl.pallas_call(functools.partial(exchange_kernel, (rep, ep, grp, half, ow...]
    add x1, other arithmetic: 0.12 us -> 0.8 us  [direct(): combine_sum = sums[0, :CAP, qw] + sums[1, CAP:2 * CAP, qw]]
    broadcast_in_dim x1, local copies, waits for them, and re-layouts: 0.08 us -> 0.7 us  [direct(): comb = jnp.broadcast_to(combined[:, None], (count, 128)).astype(BF16)]
    another operation x1, other arithmetic: 0.01 us -> 0.61 us  [direct(): jnp.stack([jnp.pad(slot_map, ((q * CAP, 12 - q * CAP), (0, 0))) for q in...]
where the time goes in v3:
time: 47.2 us; the launch traced here: 47 us
  Pallas kernels  42.4 us (90%)
  other arithmetic  3.06 us (6%)
  local copies, waits for them, and re-layouts  0.83 us (2%)
  between operations  0.67 us (1%)
    pallas_call x1, Pallas kernels, direct(): pl.pallas_call(functools.partial(exchange_kernel, (rep, ep, grp, half, ow...  36.1 us
    pallas_call x1, Pallas kernels, direct(): pl.pallas_call(contract_kernel, grid=(nch,), out_shape=(jax.ShapeDtypeStr...  6.27 us

profile of v3, /device:TPU:0, one launch (start us, length us, event | category | flops | bytes accessed | tf_op | source)
XLA Modules:
  0.0 47.0 jit_solution(16336746057692473551)
XLA Ops:
  0.6 0.7 %select_reduce_fusion = (bf16[128]{0:T(256)(128)(2,1)S(1)}, f32[128]{0:T(128)S(1)}) fusion(bf16[128,2]{0,1:T(2,128)(2,1)} %param.8, s32[128,2]{0,1:T(2,128)} %param.7), kind=kLoop, calls=%fused_computation.10 | loop fusion | flops 1280 | bytes 2304 | tf_op jit(solution)/shard_map/reduce_sum | solution.py:17
  1.3 0.7 %broadcast_in_dim.2.comb_ref = bf16[128,128]{1,0:T(8,128)(2,1)} broadcast(bf16[128]{0:T(256)(128)(2,1)S(1)} %get-tuple-element.13), dimensions={0} | broadcast | bytes 33024 | tf_op jit(solution)/shard_map/broadcast_in_dim | solution.py:325
  2.0 0.1 copy.9
  2.2 0.2 reduce-window.8
  2.3 0.1 reduce
  2.5 0.6 %pad_maximum_fusion.slots_ref = bf16[4,16,128]{2,1,0:T(8,128)(2,1)} fusion(bf16[1,16,128]{2,1,0:T(8,128)(2,1)S(1)} %get-tuple-element.16, bf16[1,16,128]{2,1,0:T(8,128)(2,1)S(1)} %get-tuple-element.17, bf16[1,16,128]{2,1,0:T(8,128)(2,1)S(1)} %get-tuple-element.18, bf16[1,16,128]{2,1,0:T(8,128)(2,1)S(1)} %get-tuple-element.15), kind=kLoop, calls=%fused_computation | loop fusion | flops 24576 | bytes 32768 | tf_op jit(solution)/shard_map/stack | solution.py:324
  3.1 0.0 copy-start
  3.1 36.1 %shard_map.76 = (bf16[4,7,3,32,256]{4,3,2,1,0:T(8,128)(2,1)}, bf16[4,8,16,128]{3,2,1,0:T(8,128)(2,1)}, f32[2,16,384]{2,1,0:T(8,128)}) custom-call(bf16[4,16,128]{2,1,0:T(8,128)(2,1)} %pad_maximum_fusion.slots_ref, bf16[128,128]{1,0:T(8,128)(2,1)} %broadcast_in_dim.2.comb_ref, bf16[128,2048]{1,0:T(8,128)(2,1)} %tok_ref.1, bf16[128,2048]{1,0:T(8,128)(2,1)} %gout_ref.1, ...), custom_call_target="tpu_custom_call" | custom-call | tf_op jit(solution)/shard_map/pallas_call | solution.py:328
  39.2 0.8 %add_reduce_fusion = f32[4]{0:T(128)S(1)} fusion(f32[2,16,384]{2,1,0:T(8,128)} %get-tuple-element.10.sum_ref), kind=kLoop, calls=%fused_computation.8 | loop fusion | flops 4 | bytes 48 | tf_op jit(solution)/shard_map/add | solution.py:377
  40.0 0.1 fusion
  40.1 0.0 copy-done
  40.1 0.6 %broadcast_select_fusion = f32[128,2]{0,1:T(2,128)} fusion(f32[128]{0:T(128)S(1)} %fusion, s32[128,2]{0,1:T(2,128)S(1)} %copy-done), kind=kLoop, calls=%fused_computation.12 | loop fusion | flops 512 | bytes 2560 | tf_op jit(solution)/shard_map/mul | solution.py:379
  40.7 6.3 %shard_map.77 = (f32[3,256,1792]{2,1,0:T(8,128)}, bf16[128,2048]{1,0:T(8,128)(2,1)}) custom-call(bf16[512,128]{1,0:T(8,128)(2,1)} %bitcast.13, bf16[4,7,3,32,256]{4,3,2,1,0:T(8,128)(2,1)} %get-tuple-element.9.hid_ref, f32[2,16,384]{2,1,0:T(8,128)} %get-tuple-element.10.sum_ref, bf16[4,16,128]{2,1,0:T(8,128)(2,1)} %pad_maximum_fusion.slots_ref), custom_call_target="tpu_custom_call" | custom-call | tf_op jit(solution)/shard_map/pallas_call | solution.py:363
  (3 shorter events, 0.0 us)
Async XLA Ops:
  3.1 37.0 %copy-start = (s32[128,2]{0,1:T(2,128)S(1)}, s32[128,2]{0,1:T(2,128)}, u32[]{:S(2)}) copy-start(s32[128,2]{0,1:T(2,128)} %param.7) | copy-start | bytes 3076
